TPU v7x, 512 devices: a whole 4x4x16 slice. The times are simulated.
512 devices in a mesh: dp: 64 (over z_lo, y, core), tile: 8 (over x, z_hi).
Axes of the slice: x: 4, y: 4, z: 16 (z_hi: 2, z_lo: 8; z = z_hi * 8 + z_lo), core: 2. Of those that a mesh axis runs over, the one named last changes fastest.
Arguments:
- frames: bfloat16 [64, 2, 3, 128, 128], P('dp', None, None, 'tile'), may hold values from 0 to 1
- features: bfloat16 [64, 64, 128, 128], P('dp', None, 'tile'), may hold values from -16 to 16
- cotangent: float32 [64, 3, 128, 128], P('dp', None, 'tile'), may hold values from -6 to 6
- head_weight: bfloat16 [108, 576], replicated, may hold values from -0.25 to 0.25
Outputs:
- grad_weight: float32 [108, 576], replicated
- grad_features: float32 [64, 64, 128, 128], P('dp', None, 'tile')
- grad_frames: float32 [64, 2, 3, 128, 128], P('dp', None, None, 'tile')
All inputs are finite; a program needn't handle non-finite values.
Results may differ from a plain program's by a relative error of at most 0.003.
Values may be sent and summed in bfloat16 or wider, within the bound.
No kernel may reach another device: no remote copies, remote signals or barrier semaphores. Data moves between devices by JAX's collectives and lax.ppermute only.
A program may use at most 64 MiB of HBM per device.

v0:
```python
import functools
import jax
import jax.numpy as jnp
from jax import lax
from jax.experimental import pallas as pl
from jax.experimental.pallas import tpu as pltpu
from jax.sharding import Mesh, PartitionSpec as P


F32, BF16 = jnp.float32, jnp.bfloat16
UNROLL_EARLY = 7
UNROLL_LATE = 7
UNROLL_FEATURE = 8
GATHER_TYPE = BF16
VMEM_GRANT = 16 * 1024 * 1024


def dims(a, b):
    return (((a,), (b,)), ((), ()))


def split(v):
    hi = v.astype(BF16)
    lo = (v - hi.astype(F32)).astype(BF16)
    return hi, lo


def column_bands(taps, width):
    rim = (taps - 1) // 2
    lane = lax.broadcasted_iota(jnp.int32, (width, width), 1)
    sub = lax.broadcasted_iota(jnp.int32, (width, width), 0)
    bands = []
    for f in range(2):
        tap = (lane - sub + (2 * width - 64 * f)) % width
        at = sub + tap - rim
        bands.append((tap < taps) & (at >= 0) & (at < width))
    return lane, sub, bands


def three_columns(row):
    lane = lax.broadcasted_iota(jnp.int32, row.shape, 1)
    width = row.shape[1]
    left = jnp.where(lane == 0, 0.0, pltpu.roll(row, 1, 1))
    right = jnp.where(lane == width - 1, 0.0, pltpu.roll(row, width - 1, 1))
    return jnp.concatenate([left, row, right], 0).astype(BF16)


def frame_terms(taps, k, g, bands):
    skew = pltpu.roll((k * taps ** -0.5).T, 0, 1, stride=1, stride_axis=0)
    out = []
    for f in range(2):
        v = k[64 * f + 32:64 * f + 64] * taps ** -0.5
        u_hi, u_lo = split(jnp.concatenate([v * g[c] for c in range(3)], 0))
        b_hi, b_lo = split(jnp.where(bands[f], skew, 0.0))
        w = jnp.dot(
            jnp.concatenate([u_hi, u_hi, u_lo], 1),
            jnp.concatenate([b_hi, b_lo, b_hi], 0), preferred_element_type=F32)
        out.append((jnp.concatenate([b_hi, b_lo], 1), jnp.concatenate([u_hi, u_lo], 0), w))
    return out


def early_kernel(taps, feat, frames, cot, wfwd, fb, bst, ust, gf, ip, fs):
    channels, rows, width = feat.shape
    rim = (taps - 1) // 2
    for n in range(6):
        ip[n] = jnp.zeros(ip.shape[1:], F32)
        ip[n, rim:rim + rows] = pltpu.roll(frames[n // 3, n % 3].astype(F32), rim + 64 * (n // 3), 1)
    fs[...] = feat[...].astype(F32).reshape(channels * rows, width)
    for y in range(rows):
        fb[y] = three_columns(fs[pl.ds(y, channels, stride=rows), :])
    gf[...] = jnp.zeros_like(gf)
    _, _, bands = column_bands(taps, width)

    def step(m, carry):
        ya = 2 * m + 1
        pair = jnp.concatenate(
            [fb[pl.ds(ya + h - 1, 3)].reshape(9 * channels, width) for h in range(2)], 1)
        k = jnp.dot(wfwd[...], pair, preferred_element_type=F32)
        for h in range(2):
            y = ya + h
            g = [cot[c, pl.ds(y, 1), :] for c in range(3)]
            terms = frame_terms(taps, k[:, width * h:width * (h + 1)], g, bands)
            for f, (b, u, w) in enumerate(terms):
                bst[y - 1, f] = b
                ust[y - 1, f] = u
                for c in range(3):
                    gf[3 * f + c, pl.ds(y, 32), :] += w[32 * c:32 * c + 32]
        return carry

    lax.fori_loop(0, rows // 2 - 1, step, 0, unroll=UNROLL_EARLY)


def late_kernel(taps, halo_up, halo_dn, cot, wfwd, fb, bst, ust, gf_in, ip_in,
                parts_ref, kgs, gf, ip, wg):
    rim = (taps - 1) // 2
    rows, channels, width = fb.shape[0], fb.shape[1] // 3, fb.shape[2]
    _, sub, bands = column_bands(taps, width)
    head = three_columns(halo_up[:channels].astype(F32))
    foot = three_columns(halo_dn[:channels].astype(F32))
    edges = jnp.concatenate([
        jnp.concatenate([head, fb[0], fb[1]], 0),
        jnp.concatenate([fb[rows - 2], fb[rows - 1], foot], 0)], 1)
    k = jnp.dot(wfwd[...], edges, preferred_element_type=F32)

    ip[...] = ip_in[...]
    for n in range(6):
        at = channels + n * rim
        turn = rim + 64 * (n // 3)
        ip[n, :rim] = pltpu.roll(halo_up[at:at + rim].astype(F32), turn, 1)
        ip[n, rim + rows:rim + rows + rim] = pltpu.roll(halo_dn[at:at + rim].astype(F32), turn, 1)
    gf[...] = gf_in[...]

    def tap_grads(y, terms):
        g = [cot[c, pl.ds(y, 1), :] for c in range(3)]
        grads = []
        horiz = None
        for f, (b, u) in enumerate(terms):
            window = jnp.concatenate(
                [ip[3 * f + c, pl.ds(y, 32), :] for c in range(3)], 0).astype(BF16)
            blended = lax.dot_general(
                jnp.concatenate([window, window], 1), b, dims(1, 1), preferred_element_type=F32)
            grads.append(sum(g[c] * blended[32 * c:32 * c + 32] for c in range(3)))
            d = lax.dot_general(
                u, jnp.concatenate([window, window], 0), dims(0, 0), preferred_element_type=F32)
            horiz = jnp.where(bands[f], d, 0.0 if f == 0 else horiz)
        turned = [horiz[:8]]
        for r in range(1, width // 8):
            turned.append(pltpu.roll(horiz[8 * r:8 * r + 8], width - 8 * r, 1))
        horiz = jnp.concatenate(turned, 0)
        for bit in range(3):
            horiz = jnp.where((sub & (1 << bit)) != 0, pltpu.roll(horiz, width - (1 << bit), 1), horiz)
        ht = horiz.T
        kg = jnp.concatenate([ht[:32], grads[0], ht[64:96], grads[1]], 0) * taps ** -0.5
        kg = kg.astype(BF16)
        kgs[y] = kg
        return kg

    pair_kg = []
    for h, y in enumerate((0, rows - 1)):
        g = [cot[c, y:y + 1, :] for c in range(3)]
        terms = frame_terms(taps, k[:, width * h:width * (h + 1)], g, bands)
        for f, (_, _, w) in enumerate(terms):
            for c in range(3):
                gf[3 * f + c, y:y + 32] += w[32 * c:32 * c + 32]
        pair_kg.append(tap_grads(y, [t[:2] for t in terms]))
    wg[...] = lax.dot_general(
        jnp.concatenate(pair_kg, 1), edges, dims(1, 1), preferred_element_type=F32)

    def step(m, carry):
        ya = 2 * m + 1
        pair = jnp.concatenate(
            [fb[pl.ds(ya + h - 1, 3)].reshape(9 * channels, width) for h in range(2)], 1)
        pair_kg = [
            tap_grads(ya + h, [(bst[ya + h - 1, f], ust[ya + h - 1, f]) for f in range(2)])
            for h in range(2)]
        wg[...] += lax.dot_general(
            jnp.concatenate(pair_kg, 1), pair, dims(1, 1), preferred_element_type=F32)
        return carry

    lax.fori_loop(0, rows // 2 - 1, step, 0, unroll=UNROLL_LATE)
    pack(wg, parts_ref, taps)


def feature_kernel(taps, kgs, gf, wbwd, gfeat, gframe, rim_up, rim_dn, acc, turned):
    rim = (taps - 1) // 2
    rows, _, width = kgs.shape
    channels = acc.shape[1]
    lane = lax.broadcasted_iota(jnp.int32, (128, width), 1)
    acc[...] = jnp.zeros_like(acc)

    def step(m, carry):
        wide = []
        for h in range(2):
            kg = kgs[2 * m + h].astype(F32)
            wide.append(jnp.concatenate([
                jnp.where(lane == width - 1, 0.0, pltpu.roll(kg, width - 1, 1)),
                kg,
                jnp.where(lane == 0, 0.0, pltpu.roll(kg, 1, 1))], 0).astype(BF16))
        part = jnp.dot(wbwd[...], jnp.concatenate(wide, 1), preferred_element_type=F32)
        for h in range(2):
            for a in range(3):
                acc[2 * m + h + a] += part[channels * a:channels * (a + 1), width * h:width * (h + 1)]
        return carry

    lax.fori_loop(0, rows // 2, step, 0, unroll=UNROLL_FEATURE)

    for y in range(rows):
        gfeat[pl.ds(y, channels, stride=rows), :] = acc[y + 1]
    rim_up[:channels] = acc[0].astype(BF16)
    rim_dn[:channels] = acc[rows + 1].astype(BF16)
    for n in range(6):
        turned[...] = pltpu.roll(gf[n], width - rim - 64 * (n // 3), 1)
        gframe[n] = turned[rim:rim + rows]
        at = channels + n * rim
        rim_up[at:at + rim] = turned[:rim].astype(BF16)
        rim_dn[at:at + rim] = turned[rim + rows:rim + rows + rim].astype(BF16)


def pack(wg, parts, taps):
    count, size, _ = parts.shape
    full, high = wg.shape[1] // 128, 4 * taps
    value = jnp.concatenate([wg[32 * g:32 * g + taps] for g in (1, 0, 3, 2)], 0)
    tail = value[:, 128 * full:]
    flat = jnp.concatenate(
        [value[:, 128 * n:128 * (n + 1)] for n in range(full)]
        + [jnp.concatenate([tail[:high // 2], tail[high // 2:]], 1)], 0)
    flat = jnp.concatenate([flat, jnp.zeros((count * size - flat.shape[0], 128), F32)], 0)
    parts[...] = flat.reshape(count, size, 128)


def unpack_kernel(taps, factor, parts, out):
    count, size, _ = parts.shape
    full, high = out.shape[1] // 128, 4 * taps
    flat = parts[...].astype(F32).reshape(count * size, 128) * factor
    for n in range(full):
        out[:, 128 * n:128 * (n + 1)] = flat[high * n:high * (n + 1)]
    tail = flat[high * full:high * full + high // 2]
    out[:, 128 * full:] = jnp.concatenate([tail[:, :64], tail[:, 64:]], 0)


def halo_kernel(taps, feat_hbm, frames_hbm, first, last, feat, frames, fs, sems):
    rim = (taps - 1) // 2
    copies = [pltpu.make_async_copy(feat_hbm, feat, sems.at[0]),
              pltpu.make_async_copy(frames_hbm, frames, sems.at[1])]
    for copy in copies:
        copy.start()
    for copy in copies:
        copy.wait()
    channels, rows, width = feat.shape
    fs[...] = feat[...].astype(F32).reshape(channels * rows, width)
    first[:channels] = fs[pl.ds(0, channels, stride=rows), :].astype(BF16)
    last[:channels] = fs[pl.ds(rows - 1, channels, stride=rows), :].astype(BF16)
    for n in range(6):
        frame = frames[n // 3, n % 3].astype(F32)
        at = channels + n * rim
        first[at:at + rim] = frame[:rim].astype(BF16)
        last[at:at + rim] = frame[rows - rim:].astype(BF16)


def order(hw, taps):
    hw = hw.reshape(2, 2, taps, -1)[:, ::-1]
    return jnp.pad(hw, ((0, 0), (0, 0), (0, 32 - taps), (0, 0))).reshape(128, -1)


def vmem_call(kernel, outs, scratch, *operands):
    vm = pl.BlockSpec(memory_space=pltpu.VMEM)
    return pl.pallas_call(
        kernel,
        out_shape=[jax.ShapeDtypeStruct(*o) for o in outs],
        in_specs=[vm] * len(operands),
        out_specs=[vm] * len(outs),
        scratch_shapes=[pltpu.VMEM(*o) for o in scratch],
        compiler_params=pltpu.CompilerParams(vmem_limit_bytes=VMEM_GRANT),
    )(*operands)


def early(feat, frames, cot, wfwd, taps):
    channels, rows, width = feat.shape
    return vmem_call(
        functools.partial(early_kernel, taps),
        [((rows, 3 * channels, width), BF16), ((rows - 2, 2, width, 2 * width), BF16),
         ((rows - 2, 2, 192, width), BF16), ((6, rows + 32, width), F32), ((6, rows + 32, width), F32)],
        [((channels * rows, width), F32)],
        feat, frames, cot, wfwd)


def late(halo_up, halo_dn, cot, wfwd, held, taps, parts):
    rows, width = held[0].shape[0], held[0].shape[2]
    columns = 3 * held[0].shape[1]
    size = -(-4 * taps * columns // (128 * parts * 8)) * 8
    return vmem_call(
        functools.partial(late_kernel, taps),
        [((parts, size, 128), F32), ((rows, 128, width), BF16), ((6, rows + 32, width), F32)],
        [((6, rows + 32, width), F32), ((128, columns), F32)],
        halo_up, halo_dn, cot, wfwd, *held)


def feature_part(kgs, gf, wbwd, taps):
    rows, _, width = kgs.shape
    channels = wbwd.shape[0] // 3
    rim_shape = ((channels + 3 * (taps - 1), width), BF16)
    return vmem_call(
        functools.partial(feature_kernel, taps),
        [((channels * rows, width), F32), ((6, rows, width), F32), rim_shape, rim_shape],
        [((rows + 2, channels, width), F32), (gf.shape[1:], F32)],
        kgs, gf, wbwd)


def halo_rows(feat, frames, taps):
    channels, rows, width = feat.shape
    shape = ((channels + 3 * (taps - 1), width), BF16)
    hbm, vm = pl.BlockSpec(memory_space=pltpu.HBM), pl.BlockSpec(memory_space=pltpu.VMEM)
    return pl.pallas_call(
        functools.partial(halo_kernel, taps),
        out_shape=[jax.ShapeDtypeStruct(*shape)] * 2,
        in_specs=[hbm, hbm],
        out_specs=[vm, vm],
        scratch_shapes=[pltpu.VMEM(feat.shape, BF16), pltpu.VMEM(frames.shape, BF16),
                        pltpu.VMEM((channels * rows, width), F32), pltpu.SemaphoreType.DMA((2,))],
    )(feat, frames)


def both_weights(hw, taps, channels):
    wfwd = order(hw, taps)
    wbwd = wfwd.reshape(128, 3, 3, channels).transpose(1, 3, 2, 0).reshape(3 * channels, 3 * 128)
    return wfwd, wbwd


def fan_kernel(parts_ref, out):
    total = jnp.sum(parts_ref[...], 0).astype(out.dtype)
    for n in range(out.shape[0]):
        out[n] = total


def fan(parts, count, dtype):
    return vmem_call(fan_kernel, [((count,) + parts.shape[1:], dtype)], [], parts)[0]


def unpack(parts, taps, columns, factor):
    return vmem_call(
        functools.partial(unpack_kernel, taps, factor), [((4 * taps, columns), F32)], [], parts)[0]


PLANE, LINE, TILE = ("y", "core", "x"), ("zl", "zh"), ("x", "zh")


def step(frames, features, cotangent, head_weight):
    taps = head_weight.shape[0] // 4
    rim = (taps - 1) // 2
    feat, frame, cot = features[0], frames[0], cotangent[0]
    channels, rows, width = feat.shape
    tiles, plane, line = lax.axis_size(TILE), lax.axis_size(PLANE), lax.axis_size(LINE)
    down = [(i, i + 1) for i in range(tiles - 1)]
    up = [(i + 1, i) for i in range(tiles - 1)]

    first, last = halo_rows(feat, frame, taps)
    halo_up = lax.ppermute(last, TILE, down)
    halo_dn = lax.ppermute(first, TILE, up)
    wfwd, wbwd = both_weights(head_weight, taps, channels)
    held = early(feat, frame, cot, wfwd, taps)
    parts, kgs, gf = late(halo_up, halo_dn, cot, wfwd, held, taps, plane)

    terms = lax.all_to_all(parts, PLANE, 0, 0)
    gfeat, gframe, rim_up, rim_dn = feature_part(kgs, gf, wbwd, taps)
    from_up = lax.ppermute(rim_dn, TILE, down)
    from_dn = lax.ppermute(rim_up, TILE, up)
    terms = lax.all_to_all(fan(terms, line, F32), LINE, 0, 0)
    total = lax.all_to_all(fan(terms, plane, GATHER_TYPE), PLANE, 0, 0)
    from_up, from_dn = from_up.astype(F32), from_dn.astype(F32)
    pixels = plane * line * rows * width
    grad_weight = unpack(total, taps, 9 * channels, pixels ** -0.5)

    gfeat = gfeat.reshape(channels, rows, width)
    gfeat = (gfeat + jnp.pad(from_up[:channels, None], ((0, 0), (0, rows - 1), (0, 0)))
             + jnp.pad(from_dn[:channels, None], ((0, 0), (rows - 1, 0), (0, 0))))
    gframe = (gframe
              + jnp.pad(from_up[channels:].reshape(6, rim, width), ((0, 0), (0, rows - rim), (0, 0)))
              + jnp.pad(from_dn[channels:].reshape(6, rim, width), ((0, 0), (rows - rim, 0), (0, 0))))
    return grad_weight, gfeat[None], gframe.reshape(1, 2, 3, rows, width)


def solution(mesh):
    fine = Mesh(mesh.devices.reshape(8, 4, 2, 4, 2), ("zl", "y", "core", "x", "zh"))
    pairs, tile = ("zl", "y", "core"), ("x", "zh")
    in_specs = (
        P(pairs, None, None, tile, None),
        P(pairs, None, tile, None),
        P(pairs, None, tile, None),
        P(),
    )
    out_specs = (P(), P(pairs, None, tile, None), P(pairs, None, None, tile, None))
    return jax.shard_map(step, mesh=fine, in_specs=in_specs, out_specs=out_specs, check_vma=False)
```

profile of v0, /device:TPU:1, one launch (start us, length us, event | category | flops | bytes accessed | tf_op | source)
XLA Modules:
  0.0 104.5 jit_solution(8849480494135992962)
XLA Ops:
  0.6 1.7 %shard_map.67 = (bf16[142,128]{1,0:T(8,128)(2,1)}, bf16[142,128]{1,0:T(8,128)(2,1)}) custom-call(bf16[64,16,128]{2,1,0:T(8,128)(2,1)} %bitcast.22, bf16[2,3,16,128]{3,2,1,0:T(8,128)(2,1)} %bitcast.28), custom_call_target="tpu_custom_call" | custom-call | tf_op jit(solution)/shard_map/pallas_call | solution.py:293
  2.3 16.3 %collective-permute-start = (bf16[142,128]{1,0:T(8,128)(2,1)}, bf16[142,128]{1,0:T(8,128)(2,1)S(1)}, u32[]{:S(2)}, u32[]{:S(2)}) collective-permute-start(bf16[142,128]{1,0:T(8,128)(2,1)} %get-tuple-element.17), channel_id=1, source_target_pairs={{0,1},{1,2},{2,3},{3,4},{4,5},{5,6},{6,7},{8,9},{9,10},{10,11},{11... | collective-permute-start | bytes 109064 | tf_op jit(solution)/shard_map/ppermute | solution.py:337
  18.6 1.3 %collective-permute-start.1 = (bf16[142,128]{1,0:T(8,128)(2,1)}, bf16[142,128]{1,0:T(8,128)(2,1)S(1)}, u32[]{:S(2)}, u32[]{:S(2)}) collective-permute-start(bf16[142,128]{1,0:T(8,128)(2,1)} %get-tuple-element.18), channel_id=1, source_target_pairs={{1,0},{2,1},{3,2},{4,3},{5,4},{6,5},{7,6},{9,8},{10,9},{11,10},{12... | collective-permute-start | bytes 109064 | tf_op jit(solution)/shard_map/ppermute | solution.py:338
  19.9 1.0 reshape.27
  20.9 0.0 copy-start
  20.9 0.9 copy-done
  21.8 0.0 copy-start.1
  21.8 0.7 copy-done.1
  22.6 0.7 copy-done.2
  23.3 4.1 %shard_map.68 = (bf16[16,192,128]{2,1,0:T(8,128)(2,1)S(1)}, bf16[14,2,128,256]{3,2,1,0:T(8,128)(2,1)S(1)}, bf16[14,2,192,128]{3,2,1,0:T(8,128)(2,1)S(1)}, f32[6,48,128]{2,1,0:T(8,128)S(1)}, f32[6,48,128]{2,1,0:T(8,128)S(1)}) custom-call(bf16[64,16,128]{2,1,0:T(8,128)(2,1)S(1)} %bitcast.23, bf16[2,3,16,128]{3,2,1,0:T(8,128)(2,1)S(1)} %bitcast.29, ...), custom_call_target="tpu_custom_call" | custom-call | tf_op jit(solution)/shard_map/pallas_call | solution.py:247
  27.4 0.0 collective-permute-done.halo_up
  27.4 4.8 %collective-permute-done.1.halo_dn = bf16[142,128]{1,0:T(8,128)(2,1)S(1)} collective-permute-done((bf16[142,128]{1,0:T(8,128)(2,1)}, bf16[142,128]{1,0:T(8,128)(2,1)S(1)}, u32[]{:S(2)}, u32[]{:S(2)}) %collective-permute-start.1) | collective-permute-done | bytes 36384 | tf_op jit(solution)/shard_map/ppermute | solution.py:338
  32.2 6.7 %shard_map.69 = (f32[32,16,128]{2,1,0:T(8,128)}, bf16[16,128,128]{2,1,0:T(8,128)(2,1)S(1)}, f32[6,48,128]{2,1,0:T(8,128)S(1)}) custom-call(bf16[142,128]{1,0:T(8,128)(2,1)S(1)} %collective-permute-done.halo_up, bf16[142,128]{1,0:T(8,128)(2,1)S(1)} %collective-permute-done.1.halo_dn, f32[3,16,128]{2,1,0:T(8,128)S(1)} %bitcast.27, ...), custom_call_target="tpu_custom_call" | custom-call | tf_op jit(solution)/shard_map/pallas_call | solution.py:247
  38.9 11.0 %all-to-all-start = ((f32[32,16,128]{2,1,0:T(8,128)}), f32[32,16,128]{2,1,0:T(8,128)S(1)}, u32[]{:S(2)}, u32[]{:S(2)}) async-start(f32[32,16,128]{2,1,0:T(8,128)} %get-tuple-element.24), calls=%async_computation | async-start | bytes 524288 | tf_op jit(solution)/shard_map/all_to_all | solution.py:343
  49.9 0.2 reshape_reshape.3
  50.1 0.3 copy.8
  50.4 0.7 shard_map.73
  51.2 1.3 %collective-permute-start.3 = (bf16[142,128]{1,0:T(8,128)(2,1)S(1)}, bf16[142,128]{1,0:T(8,128)(2,1)S(1)}, u32[]{:S(2)}, u32[]{:S(2)}) collective-permute-start(bf16[142,128]{1,0:T(8,128)(2,1)S(1)} %get-tuple-element.29), channel_id=1, source_target_pairs={{1,0},{2,1},{3,2},{4,3},{5,4},{6,5},{7,6},{9,8},{10,9},{11,10},{12... | collective-permute-start | bytes 109064 | tf_op jit(solution)/shard_map/ppermute | solution.py:346
  52.5 12.7 %collective-permute-start.2 = (bf16[142,128]{1,0:T(8,128)(2,1)S(1)}, bf16[142,128]{1,0:T(8,128)(2,1)S(1)}, u32[]{:S(2)}, u32[]{:S(2)}) collective-permute-start(bf16[142,128]{1,0:T(8,128)(2,1)S(1)} %get-tuple-element.28), channel_id=1, source_target_pairs={{0,1},{1,2},{2,3},{3,4},{4,5},{5,6},{6,7},{8,9},{9,10},{10,11},{11... | collective-permute-start | bytes 109064 | tf_op jit(solution)/shard_map/ppermute | solution.py:345
  65.2 0.0 collective-permute-done.3
  65.2 0.0 all-to-all-done.parts_ref
  65.2 0.7 shard_map.70
  65.9 5.6 %all-to-all-start.1 = ((f32[16,16,128]{2,1,0:T(8,128)}), f32[16,16,128]{2,1,0:T(8,128)S(1)}, u32[]{:S(2)}, u32[]{:S(2)}) async-start(f32[16,16,128]{2,1,0:T(8,128)} %shard_map.70), calls=%async_computation.1 | async-start | bytes 262144 | tf_op jit(solution)/shard_map/all_to_all | solution.py:347
  71.5 0.0 collective-permute-done.2
  71.6 0.2 fusion.1
  71.8 1.1 %copy.10 = f32[1,64,16,128]{3,2,1,0:T(8,128)} copy(f32[1,64,16,128]{3,1,2,0:T(8,128)S(1)} %fusion.1) | data formatting | bytes 1048576
  72.9 12.0 %all-to-all-done.1.parts_ref = f32[16,16,128]{2,1,0:T(8,128)S(1)} async-done(((f32[16,16,128]{2,1,0:T(8,128)}), f32[16,16,128]{2,1,0:T(8,128)S(1)}, u32[]{:S(2)}, u32[]{:S(2)}) %all-to-all-start.1) | async-done | bytes 131104 | tf_op jit(solution)/shard_map/all_to_all | solution.py:347
  84.9 0.7 shard_map.71
  85.6 10.5 %all-to-all-start.2 = ((bf16[32,16,128]{2,1,0:T(8,128)(2,1)}), bf16[32,16,128]{2,1,0:T(8,128)(2,1)S(1)}, u32[]{:S(2)}, u32[]{:S(2)}) async-start(bf16[32,16,128]{2,1,0:T(8,128)(2,1)} %shard_map.71), calls=%async_computation.2 | async-start | bytes 262144 | tf_op jit(solution)/shard_map/all_to_all | solution.py:348
  96.1 0.6 pad_add_fusion
  96.7 7.0 %all-to-all-done.2.parts = bf16[32,16,128]{2,1,0:T(8,128)(2,1)S(1)} async-done(((bf16[32,16,128]{2,1,0:T(8,128)(2,1)}), bf16[32,16,128]{2,1,0:T(8,128)(2,1)S(1)}, u32[]{:S(2)}, u32[]{:S(2)}) %all-to-all-start.2) | async-done | bytes 131104 | tf_op jit(solution)/shard_map/all_to_all | solution.py:348
  103.7 0.8 shard_map.72
  (12 shorter events, 0.1 us)
Async XLA Ops:
  2.3 25.1 %collective-permute-start = (bf16[142,128]{1,0:T(8,128)(2,1)}, bf16[142,128]{1,0:T(8,128)(2,1)S(1)}, u32[]{:S(2)}, u32[]{:S(2)}) collective-permute-start(bf16[142,128]{1,0:T(8,128)(2,1)} %get-tuple-element.17), channel_id=1, source_target_pairs={{0,1},{1,2},{2,3},{3,4},{4,5},{5,6},{6,7},{8,9},{9,10},{10,11},{11... | collective-permute-start | bytes 109064 | tf_op jit(solution)/shard_map/ppermute | solution.py:337
  18.6 13.6 %collective-permute-start.1 = (bf16[142,128]{1,0:T(8,128)(2,1)}, bf16[142,128]{1,0:T(8,128)(2,1)S(1)}, u32[]{:S(2)}, u32[]{:S(2)}) collective-permute-start(bf16[142,128]{1,0:T(8,128)(2,1)} %get-tuple-element.18), channel_id=1, source_target_pairs={{1,0},{2,1},{3,2},{4,3},{5,4},{6,5},{7,6},{9,8},{10,9},{11,10},{12... | collective-permute-start | bytes 109064 | tf_op jit(solution)/shard_map/ppermute | solution.py:338
  20.9 1.0 copy-start
  21.8 0.7 copy-start.1
  22.6 0.7 copy-start.2
  38.9 26.3 %all-to-all-start = ((f32[32,16,128]{2,1,0:T(8,128)}), f32[32,16,128]{2,1,0:T(8,128)S(1)}, u32[]{:S(2)}, u32[]{:S(2)}) async-start(f32[32,16,128]{2,1,0:T(8,128)} %get-tuple-element.24), calls=%async_computation | async-start | bytes 524288 | tf_op jit(solution)/shard_map/all_to_all | solution.py:343
  51.2 14.0 %collective-permute-start.3 = (bf16[142,128]{1,0:T(8,128)(2,1)S(1)}, bf16[142,128]{1,0:T(8,128)(2,1)S(1)}, u32[]{:S(2)}, u32[]{:S(2)}) collective-permute-start(bf16[142,128]{1,0:T(8,128)(2,1)S(1)} %get-tuple-element.29), channel_id=1, source_target_pairs={{1,0},{2,1},{3,2},{4,3},{5,4},{6,5},{7,6},{9,8},{10,9},{11,10},{12... | collective-permute-start | bytes 109064 | tf_op jit(solution)/shard_map/ppermute | solution.py:346
  52.5 19.1 %collective-permute-start.2 = (bf16[142,128]{1,0:T(8,128)(2,1)S(1)}, bf16[142,128]{1,0:T(8,128)(2,1)S(1)}, u32[]{:S(2)}, u32[]{:S(2)}) collective-permute-start(bf16[142,128]{1,0:T(8,128)(2,1)S(1)} %get-tuple-element.28), channel_id=1, source_target_pairs={{0,1},{1,2},{2,3},{3,4},{4,5},{5,6},{6,7},{8,9},{9,10},{10,11},{11... | collective-permute-start | bytes 109064 | tf_op jit(solution)/shard_map/ppermute | solution.py:345
  65.9 19.0 %all-to-all-start.1 = ((f32[16,16,128]{2,1,0:T(8,128)}), f32[16,16,128]{2,1,0:T(8,128)S(1)}, u32[]{:S(2)}, u32[]{:S(2)}) async-start(f32[16,16,128]{2,1,0:T(8,128)} %shard_map.70), calls=%async_computation.1 | async-start | bytes 262144 | tf_op jit(solution)/shard_map/all_to_all | solution.py:347
  85.6 18.1 %all-to-all-start.2 = ((bf16[32,16,128]{2,1,0:T(8,128)(2,1)}), bf16[32,16,128]{2,1,0:T(8,128)(2,1)S(1)}, u32[]{:S(2)}, u32[]{:S(2)}) async-start(bf16[32,16,128]{2,1,0:T(8,128)(2,1)} %shard_map.71), calls=%async_computation.2 | async-start | bytes 262144 | tf_op jit(solution)/shard_map/all_to_all | solution.py:348
where the time goes:
time: 105 us; the launch traced here: 104 us
  starting transfers between devices  58.6 us (56%)
  waiting for transfers between devices  23.8 us (23%)
  Pallas kernels  15.3 us (15%)
  local copies, waits for them, and re-layouts  5.07 us (5%)
    ppermute x1, starting transfers between devices, step(): halo_up = lax.ppermute(last, TILE, down)  16.3 us
    pallas_call x6, Pallas kernels, vmem_call(): pl.pallas_call(kernel, out_shape=[jax.ShapeDtypeStruct(*o) for o in outs]...  13.6 us
    ppermute x1, starting transfers between devices, step(): from_up = lax.ppermute(rim_dn, TILE, down)  12.7 us
    all_to_all x1, waiting for transfers between devices, step(): terms = lax.all_to_all(fan(terms, line, F32), LINE, 0, 0)  12 us
    all_to_all x1, starting transfers between devices, step(): terms = lax.all_to_all(parts, PLANE, 0, 0)  11 us
    all_to_all x1, starting transfers between devices, step(): total = lax.all_to_all(fan(terms, plane, GATHER_TYPE), PLANE, 0, 0)  10.5 us
    all_to_all x1, waiting for transfers between devices, step(): total = lax.all_to_all(fan(terms, plane, GATHER_TYPE), PLANE, 0, 0)  6.97 us
    all_to_all x1, starting transfers between devices, step(): terms = lax.all_to_all(fan(terms, line, F32), LINE, 0, 0)  5.62 us
  transfers between devices with their start and end apart: 7, of which 3 were waited for; matrix products, arithmetic and copies ran while one was open for 3% of the time, Pallas kernels for 5%

commit v1 on v0

--- a/solution.py
+++ b/solution.py
@@ -161,7 +161,7 @@
     pack(wg, parts_ref, taps)
 
 
-def feature_kernel(taps, kgs, gf, wbwd, gfeat, gframe, rim_up, rim_dn, acc, turned):
+def feature_kernel(taps, half, kgs, gf, wbwd, gfeat, gframe, rims, acc, turned):
     rim = (taps - 1) // 2
     rows, _, width = kgs.shape
     channels = acc.shape[1]
@@ -186,14 +186,15 @@
 
     for y in range(rows):
         gfeat[pl.ds(y, channels, stride=rows), :] = acc[y + 1]
-    rim_up[:channels] = acc[0].astype(BF16)
-    rim_dn[:channels] = acc[rows + 1].astype(BF16)
+    up, dn = 1 - half[0], half[0]
+    rims[up, :channels] = acc[0].astype(BF16)
+    rims[dn, :channels] = acc[rows + 1].astype(BF16)
     for n in range(6):
         turned[...] = pltpu.roll(gf[n], width - rim - 64 * (n // 3), 1)
         gframe[n] = turned[rim:rim + rows]
         at = channels + n * rim
-        rim_up[at:at + rim] = turned[:rim].astype(BF16)
-        rim_dn[at:at + rim] = turned[rim + rows:rim + rows + rim].astype(BF16)
+        rims[up, at:at + rim] = turned[:rim].astype(BF16)
+        rims[dn, at:at + rim] = turned[rim + rows:rim + rows + rim].astype(BF16)
 
 
 def pack(wg, parts, taps):
@@ -275,15 +276,20 @@
         halo_up, halo_dn, cot, wfwd, *held)
 
 
-def feature_part(kgs, gf, wbwd, taps):
+def feature_part(half, kgs, gf, wbwd, taps):
     rows, _, width = kgs.shape
     channels = wbwd.shape[0] // 3
-    rim_shape = ((channels + 3 * (taps - 1), width), BF16)
-    return vmem_call(
+    vm = pl.BlockSpec(memory_space=pltpu.VMEM)
+    return pl.pallas_call(
         functools.partial(feature_kernel, taps),
-        [((channels * rows, width), F32), ((6, rows, width), F32), rim_shape, rim_shape],
-        [((rows + 2, channels, width), F32), (gf.shape[1:], F32)],
-        kgs, gf, wbwd)
+        out_shape=[jax.ShapeDtypeStruct((channels * rows, width), F32),
+                   jax.ShapeDtypeStruct((6, rows, width), F32),
+                   jax.ShapeDtypeStruct((2, channels + 3 * (taps - 1), width), BF16)],
+        in_specs=[pl.BlockSpec(memory_space=pltpu.SMEM), vm, vm, vm],
+        out_specs=[vm] * 3,
+        scratch_shapes=[pltpu.VMEM((rows + 2, channels, width), F32), pltpu.VMEM(gf.shape[1:], F32)],
+        compiler_params=pltpu.CompilerParams(vmem_limit_bytes=VMEM_GRANT),
+    )(half, kgs, gf, wbwd)
 
 
 def halo_rows(feat, frames, taps):
@@ -341,12 +347,16 @@
     parts, kgs, gf = late(halo_up, halo_dn, cot, wfwd, held, taps, plane)
 
     terms = lax.all_to_all(parts, PLANE, 0, 0)
-    gfeat, gframe, rim_up, rim_dn = feature_part(kgs, gf, wbwd, taps)
-    from_up = lax.ppermute(rim_dn, TILE, down)
-    from_dn = lax.ppermute(rim_up, TILE, up)
+    half = lax.axis_index("zh")
+    gfeat, gframe, rims = feature_part(half.reshape(1), kgs, gf, wbwd, taps)
+    rims = lax.ppermute(rims, TILE, [(i, i ^ 1) for i in range(tiles)])
+    near = rims[0]
+    far = lax.ppermute(rims[1], TILE, [(i, i + 2) for i in range(0, tiles - 2, 2)]
+                       + [(i, i - 2) for i in range(3, tiles, 2)])
     terms = lax.all_to_all(fan(terms, line, F32), LINE, 0, 0)
     total = lax.all_to_all(fan(terms, plane, GATHER_TYPE), PLANE, 0, 0)
-    from_up, from_dn = from_up.astype(F32), from_dn.astype(F32)
+    from_up = jnp.where(half == 0, far, near).astype(F32)
+    from_dn = jnp.where(half == 0, near, far).astype(F32)
     pixels = plane * line * rows * width
     grad_weight = unpack(total, taps, 9 * channels, pixels ** -0.5)
 

time: 105 us -> 103 us (0.981)
  waiting for transfers between devices: 23.8 us -> 31.3 us
  starting transfers between devices: 58.6 us -> 51.9 us
  local copies, waits for them, and re-layouts: 5.07 us -> 2.66 us
    all_to_all x1, waiting for transfers between devices: 0.01 us -> 5.58 us  [step(): terms = lax.all_to_all(parts, PLANE, 0, 0)]
    ppermute x2, starting transfers between devices: 14 us -> 9.33 us  [the longest x1 6.07 us: step(): rims = lax.ppermute(rims, TILE, [(i, i ^ 1) for i in range(tiles)])]
    all_to_all x1, starting transfers between devices: 5.62 us -> 10.1 us  [step(): terms = lax.all_to_all(fan(terms, line, F32), LINE, 0, 0)]
    all_to_all x1, starting transfers between devices: 10.5 us -> 6.33 us  [step(): total = lax.all_to_all(fan(terms, plane, GATHER_TYPE), PLANE, 0, 0)]
    unnamed x8, local copies, waits for them, and re-layouts: 3.54 us -> 1.14 us
    all_to_all x1, starting transfers between devices: 11 us -> 8.62 us  [step(): terms = lax.all_to_all(parts, PLANE, 0, 0)]
    ppermute x1, waiting for transfers between devices: 4.79 us -> 6.65 us  [step(): halo_dn = lax.ppermute(first, TILE, up)]
    pallas_call x6 -> x5, Pallas kernels: 13.6 us -> 12.9 us  [vmem_call(): pl.pallas_call(kernel, out_shape=[jax.ShapeDtypeStruct(*o) for o in outs]...]
  transfers between devices with their start and end apart: 7 -> 7, of which waited for: 3 -> 4; matrix products, arithmetic and copies ran while one was open for 3% -> 3% of each run, Pallas kernels for 5% -> 5%
where the time goes in v1:
time: 103 us
  starting transfers between devices  51.9 us (50%)
  waiting for transfers between devices  31.3 us (30%)
  Pallas kernels  15.4 us (15%)
  local copies, waits for them, and re-layouts  2.66 us (3%)
    ppermute x1, starting transfers between devices, step(): halo_up = lax.ppermute(last, TILE, down)  16.3 us
    pallas_call x5, Pallas kernels, vmem_call(): pl.pallas_call(kernel, out_shape=[jax.ShapeDtypeStruct(*o) for o in outs]...  12.9 us
    all_to_all x1, waiting for transfers between devices, step(): terms = lax.all_to_all(fan(terms, line, F32), LINE, 0, 0)  12 us
    all_to_all x1, starting transfers between devices, step(): terms = lax.all_to_all(fan(terms, line, F32), LINE, 0, 0)  10.1 us
    all_to_all x1, starting transfers between devices, step(): terms = lax.all_to_all(parts, PLANE, 0, 0)  8.62 us
    all_to_all x1, waiting for transfers between devices, step(): total = lax.all_to_all(fan(terms, plane, GATHER_TYPE), PLANE, 0, 0)  7.06 us
    ppermute x1, waiting for transfers between devices, step(): halo_dn = lax.ppermute(first, TILE, up)  6.65 us
    all_to_all x1, starting transfers between devices, step(): total = lax.all_to_all(fan(terms, plane, GATHER_TYPE), PLANE, 0, 0)  6.33 us
  transfers between devices with their start and end apart: 7, of which 4 were waited for; matrix products, arithmetic and copies ran while one was open for 3% of the time, Pallas kernels for 5%

profile of v1, /device:TPU:1, one launch (start us, length us, event | category | flops | bytes accessed | tf_op | source)
XLA Modules:
  0.0 103.0 jit_solution(847700681482155032)
XLA Ops:
  0.6 0.0 copy-start
  0.6 0.0 copy-start.2
  0.7 0.0 copy-start.1
  0.7 1.7 %shard_map.67 = (bf16[142,128]{1,0:T(8,128)(2,1)}, bf16[142,128]{1,0:T(8,128)(2,1)}) custom-call(bf16[64,16,128]{2,1,0:T(8,128)(2,1)} %bitcast.31, bf16[2,3,16,128]{3,2,1,0:T(8,128)(2,1)} %bitcast.37), custom_call_target="tpu_custom_call" | custom-call | tf_op jit(solution)/shard_map/pallas_call | solution.py:299
  2.4 16.3 %collective-permute-start = (bf16[142,128]{1,0:T(8,128)(2,1)}, bf16[142,128]{1,0:T(8,128)(2,1)S(1)}, u32[]{:S(2)}, u32[]{:S(2)}) collective-permute-start(bf16[142,128]{1,0:T(8,128)(2,1)} %get-tuple-element.16), channel_id=1, source_target_pairs={{0,1},{1,2},{2,3},{3,4},{4,5},{5,6},{6,7},{8,9},{9,10},{10,11},{11... | collective-permute-start | bytes 109064 | tf_op jit(solution)/shard_map/ppermute | solution.py:343
  18.6 1.3 %collective-permute-start.1 = (bf16[142,128]{1,0:T(8,128)(2,1)}, bf16[142,128]{1,0:T(8,128)(2,1)S(1)}, u32[]{:S(2)}, u32[]{:S(2)}) collective-permute-start(bf16[142,128]{1,0:T(8,128)(2,1)} %get-tuple-element.17), channel_id=1, source_target_pairs={{1,0},{2,1},{3,2},{4,3},{5,4},{6,5},{7,6},{9,8},{10,9},{11,10},{12... | collective-permute-start | bytes 109064 | tf_op jit(solution)/shard_map/ppermute | solution.py:344
  20.0 1.0 reshape.30
  21.0 0.2 reshape_reshape.3
  21.2 0.3 copy.8
  21.5 0.0 copy-done
  21.5 0.0 copy-done.2
  21.5 4.1 %shard_map.68 = (bf16[16,192,128]{2,1,0:T(8,128)(2,1)S(1)}, bf16[14,2,128,256]{3,2,1,0:T(8,128)(2,1)S(1)}, bf16[14,2,192,128]{3,2,1,0:T(8,128)(2,1)S(1)}, f32[6,48,128]{2,1,0:T(8,128)S(1)}, f32[6,48,128]{2,1,0:T(8,128)S(1)}) custom-call(bf16[64,16,128]{2,1,0:T(8,128)(2,1)S(1)} %bitcast.32, bf16[2,3,16,128]{3,2,1,0:T(8,128)(2,1)S(1)} %bitcast.38, ...), custom_call_target="tpu_custom_call" | custom-call | tf_op jit(solution)/shard_map/pallas_call | solution.py:248
  25.6 0.0 collective-permute-done.halo_up
  25.6 6.7 %collective-permute-done.1.halo_dn = bf16[142,128]{1,0:T(8,128)(2,1)S(1)} collective-permute-done((bf16[142,128]{1,0:T(8,128)(2,1)}, bf16[142,128]{1,0:T(8,128)(2,1)S(1)}, u32[]{:S(2)}, u32[]{:S(2)}) %collective-permute-start.1) | collective-permute-done | bytes 36384 | tf_op jit(solution)/shard_map/ppermute | solution.py:344
  32.3 6.7 %shard_map.69 = (f32[32,16,128]{2,1,0:T(8,128)}, bf16[16,128,128]{2,1,0:T(8,128)(2,1)S(1)}, f32[6,48,128]{2,1,0:T(8,128)S(1)}) custom-call(bf16[142,128]{1,0:T(8,128)(2,1)S(1)} %collective-permute-done.halo_up, bf16[142,128]{1,0:T(8,128)(2,1)S(1)} %collective-permute-done.1.halo_dn, f32[3,16,128]{2,1,0:T(8,128)S(1)} %bitcast.36, ...), custom_call_target="tpu_custom_call" | custom-call | tf_op jit(solution)/shard_map/pallas_call | solution.py:248
  38.9 0.7 shard_map.73
  39.7 6.1 %collective-permute-start.2 = (bf16[2,142,128]{2,1,0:T(8,128)(2,1)S(1)}, bf16[2,142,128]{2,1,0:T(8,128)(2,1)S(1)}, u32[]{:S(2)}, u32[]{:S(2)}) collective-permute-start(bf16[2,142,128]{2,1,0:T(8,128)(2,1)S(1)} %get-tuple-element.27), channel_id=1, source_target_pairs={{0,1},{1,0},{2,3},{3,2},{4,5},{5,4},{6,7},{7,6},{8,9},{9,8},{10,11... | collective-permute-start | bytes 218120 | tf_op jit(solution)/shard_map/ppermute | solution.py:352
  45.8 8.6 %all-to-all-start = ((f32[32,16,128]{2,1,0:T(8,128)}), f32[32,16,128]{2,1,0:T(8,128)S(1)}, u32[]{:S(2)}, u32[]{:S(2)}) async-start(f32[32,16,128]{2,1,0:T(8,128)} %get-tuple-element.23), calls=%async_computation | async-start | bytes 524288 | tf_op jit(solution)/shard_map/all_to_all | solution.py:349
  54.4 0.0 collective-permute-done.2
  54.4 3.3 %collective-permute-start.3 = (bf16[142,128]{1,0:T(8,128)(2,1)S(1)}, bf16[142,128]{1,0:T(8,128)(2,1)S(1)}, u32[]{:S(2)}, u32[]{:S(2)}) collective-permute-start(bf16[142,128]{1,0:T(8,128)(2,1)S(1)} %slice_bitcast_fusion.1), channel_id=1, source_target_pairs={{0,2},{2,4},{4,6},{3,1},{5,3},{7,5},{8,10},{10,12},{12,14},{11,9},... | collective-permute-start | bytes 109064 | tf_op jit(solution)/shard_map/ppermute | solution.py:354
  57.7 5.6 %all-to-all-done.parts_ref = f32[32,16,128]{2,1,0:T(8,128)S(1)} async-done(((f32[32,16,128]{2,1,0:T(8,128)}), f32[32,16,128]{2,1,0:T(8,128)S(1)}, u32[]{:S(2)}, u32[]{:S(2)}) %all-to-all-start) | async-done | bytes 262176 | tf_op jit(solution)/shard_map/all_to_all | solution.py:349
  63.3 0.7 shard_map.70
  64.0 10.1 %all-to-all-start.1 = ((f32[16,16,128]{2,1,0:T(8,128)}), f32[16,16,128]{2,1,0:T(8,128)S(1)}, u32[]{:S(2)}, u32[]{:S(2)}) async-start(f32[16,16,128]{2,1,0:T(8,128)} %shard_map.70), calls=%async_computation.1 | async-start | bytes 262144 | tf_op jit(solution)/shard_map/all_to_all | solution.py:356
  74.1 0.0 collective-permute-done.3
  74.2 0.2 fusion.1
  74.3 1.1 %copy.10 = f32[1,64,16,128]{3,2,1,0:T(8,128)} copy(f32[1,64,16,128]{3,1,2,0:T(8,128)S(1)} %fusion.1) | data formatting | bytes 1048576
  75.5 12.0 %all-to-all-done.1.parts_ref = f32[16,16,128]{2,1,0:T(8,128)S(1)} async-done(((f32[16,16,128]{2,1,0:T(8,128)}), f32[16,16,128]{2,1,0:T(8,128)S(1)}, u32[]{:S(2)}, u32[]{:S(2)}) %all-to-all-start.1) | async-done | bytes 131104 | tf_op jit(solution)/shard_map/all_to_all | solution.py:356
  87.5 0.7 shard_map.71
  88.2 6.3 %all-to-all-start.2 = ((bf16[32,16,128]{2,1,0:T(8,128)(2,1)}), bf16[32,16,128]{2,1,0:T(8,128)(2,1)S(1)}, u32[]{:S(2)}, u32[]{:S(2)}) async-start(bf16[32,16,128]{2,1,0:T(8,128)(2,1)} %shard_map.71), calls=%async_computation.2 | async-start | bytes 262144 | tf_op jit(solution)/shard_map/all_to_all | solution.py:357
  94.5 0.6 pad_add_fusion
  95.1 7.1 %all-to-all-done.2.parts = bf16[32,16,128]{2,1,0:T(8,128)(2,1)S(1)} async-done(((bf16[32,16,128]{2,1,0:T(8,128)(2,1)}), bf16[32,16,128]{2,1,0:T(8,128)(2,1)S(1)}, u32[]{:S(2)}, u32[]{:S(2)}) %all-to-all-start.2) | async-done | bytes 131104 | tf_op jit(solution)/shard_map/all_to_all | solution.py:357
  102.2 0.8 shard_map.72
  (11 shorter events, 0.1 us)
Async XLA Ops:
  0.6 20.9 %copy-start = (bf16[1,64,16,128]{3,2,1,0:T(8,128)(2,1)S(1)}, bf16[1,64,16,128]{3,2,1,0:T(8,128)(2,1)}, u32[]{:S(2)}) copy-start(bf16[1,64,16,128]{3,2,1,0:T(8,128)(2,1)} %param.5) | copy-start | bytes 786436
  0.6 20.9 %copy-start.2 = (bf16[1,2,3,16,128]{4,3,2,1,0:T(8,128)(2,1)S(1)}, bf16[1,2,3,16,128]{4,3,2,1,0:T(8,128)(2,1)}, u32[]{:S(2)}) copy-start(bf16[1,2,3,16,128]{4,3,2,1,0:T(8,128)(2,1)} %param.4) | copy-start | bytes 73732
  0.7 20.9 %copy-start.1 = (f32[1,3,16,128]{3,2,1,0:T(8,128)S(1)}, f32[1,3,16,128]{3,2,1,0:T(8,128)}, u32[]{:S(2)}) copy-start(f32[1,3,16,128]{3,2,1,0:T(8,128)} %param.6) | copy-start | bytes 73732
  2.4 23.2 %collective-permute-start = (bf16[142,128]{1,0:T(8,128)(2,1)}, bf16[142,128]{1,0:T(8,128)(2,1)S(1)}, u32[]{:S(2)}, u32[]{:S(2)}) collective-permute-start(bf16[142,128]{1,0:T(8,128)(2,1)} %get-tuple-element.16), channel_id=1, source_target_pairs={{0,1},{1,2},{2,3},{3,4},{4,5},{5,6},{6,7},{8,9},{9,10},{10,11},{11... | collective-permute-start | bytes 109064 | tf_op jit(solution)/shard_map/ppermute | solution.py:343
  18.6 13.6 %collective-permute-start.1 = (bf16[142,128]{1,0:T(8,128)(2,1)}, bf16[142,128]{1,0:T(8,128)(2,1)S(1)}, u32[]{:S(2)}, u32[]{:S(2)}) collective-permute-start(bf16[142,128]{1,0:T(8,128)(2,1)} %get-tuple-element.17), channel_id=1, source_target_pairs={{1,0},{2,1},{3,2},{4,3},{5,4},{6,5},{7,6},{9,8},{10,9},{11,10},{12... | collective-permute-start | bytes 109064 | tf_op jit(solution)/shard_map/ppermute | solution.py:344
  39.7 14.7 %collective-permute-start.2 = (bf16[2,142,128]{2,1,0:T(8,128)(2,1)S(1)}, bf16[2,142,128]{2,1,0:T(8,128)(2,1)S(1)}, u32[]{:S(2)}, u32[]{:S(2)}) collective-permute-start(bf16[2,142,128]{2,1,0:T(8,128)(2,1)S(1)} %get-tuple-element.27), channel_id=1, source_target_pairs={{0,1},{1,0},{2,3},{3,2},{4,5},{5,4},{6,7},{7,6},{8,9},{9,8},{10,11... | collective-permute-start | bytes 218120 | tf_op jit(solution)/shard_map/ppermute | solution.py:352
  45.8 17.5 %all-to-all-start = ((f32[32,16,128]{2,1,0:T(8,128)}), f32[32,16,128]{2,1,0:T(8,128)S(1)}, u32[]{:S(2)}, u32[]{:S(2)}) async-start(f32[32,16,128]{2,1,0:T(8,128)} %get-tuple-element.23), calls=%async_computation | async-start | bytes 524288 | tf_op jit(solution)/shard_map/all_to_all | solution.py:349
  54.4 19.7 %collective-permute-start.3 = (bf16[142,128]{1,0:T(8,128)(2,1)S(1)}, bf16[142,128]{1,0:T(8,128)(2,1)S(1)}, u32[]{:S(2)}, u32[]{:S(2)}) collective-permute-start(bf16[142,128]{1,0:T(8,128)(2,1)S(1)} %slice_bitcast_fusion.1), channel_id=1, source_target_pairs={{0,2},{2,4},{4,6},{3,1},{5,3},{7,5},{8,10},{10,12},{12,14},{11,9},... | collective-permute-start | bytes 109064 | tf_op jit(solution)/shard_map/ppermute | solution.py:354
  64.0 23.5 %all-to-all-start.1 = ((f32[16,16,128]{2,1,0:T(8,128)}), f32[16,16,128]{2,1,0:T(8,128)S(1)}, u32[]{:S(2)}, u32[]{:S(2)}) async-start(f32[16,16,128]{2,1,0:T(8,128)} %shard_map.70), calls=%async_computation.1 | async-start | bytes 262144 | tf_op jit(solution)/shard_map/all_to_all | solution.py:356
  88.2 14.0 %all-to-all-start.2 = ((bf16[32,16,128]{2,1,0:T(8,128)(2,1)}), bf16[32,16,128]{2,1,0:T(8,128)(2,1)S(1)}, u32[]{:S(2)}, u32[]{:S(2)}) async-start(bf16[32,16,128]{2,1,0:T(8,128)(2,1)} %shard_map.71), calls=%async_computation.2 | async-start | bytes 262144 | tf_op jit(solution)/shard_map/all_to_all | solution.py:357

commit v2 on v1

--- a/solution.py
+++ b/solution.py
@@ -161,7 +161,7 @@
     pack(wg, parts_ref, taps)
 
 
-def feature_kernel(taps, half, kgs, gf, wbwd, gfeat, gframe, rims, acc, turned):
+def feature_kernel(taps, half, kgs, gf, wbwd, gfeat, gframe, near, far, acc, turned, rims):
     rim = (taps - 1) // 2
     rows, _, width = kgs.shape
     channels = acc.shape[1]
@@ -195,6 +195,8 @@
         at = channels + n * rim
         rims[up, at:at + rim] = turned[:rim].astype(BF16)
         rims[dn, at:at + rim] = turned[rim + rows:rim + rows + rim].astype(BF16)
+    near[...] = rims[0]
+    far[...] = rims[1]
 
 
 def pack(wg, parts, taps):
@@ -280,14 +282,16 @@
     rows, _, width = kgs.shape
     channels = wbwd.shape[0] // 3
     vm = pl.BlockSpec(memory_space=pltpu.VMEM)
+    rim_shape = (channels + 3 * (taps - 1), width)
     return pl.pallas_call(
         functools.partial(feature_kernel, taps),
         out_shape=[jax.ShapeDtypeStruct((channels * rows, width), F32),
                    jax.ShapeDtypeStruct((6, rows, width), F32),
-                   jax.ShapeDtypeStruct((2, channels + 3 * (taps - 1), width), BF16)],
+                   jax.ShapeDtypeStruct(rim_shape, BF16), jax.ShapeDtypeStruct(rim_shape, BF16)],
         in_specs=[pl.BlockSpec(memory_space=pltpu.SMEM), vm, vm, vm],
-        out_specs=[vm] * 3,
-        scratch_shapes=[pltpu.VMEM((rows + 2, channels, width), F32), pltpu.VMEM(gf.shape[1:], F32)],
+        out_specs=[vm] * 4,
+        scratch_shapes=[pltpu.VMEM((rows + 2, channels, width), F32), pltpu.VMEM(gf.shape[1:], F32),
+                        pltpu.VMEM((2,) + rim_shape, BF16)],
         compiler_params=pltpu.CompilerParams(vmem_limit_bytes=VMEM_GRANT),
     )(half, kgs, gf, wbwd)
 
@@ -348,11 +352,11 @@
 
     terms = lax.all_to_all(parts, PLANE, 0, 0)
     half = lax.axis_index("zh")
-    gfeat, gframe, rims = feature_part(half.reshape(1), kgs, gf, wbwd, taps)
-    rims = lax.ppermute(rims, TILE, [(i, i ^ 1) for i in range(tiles)])
-    near = rims[0]
-    far = lax.ppermute(rims[1], TILE, [(i, i + 2) for i in range(0, tiles - 2, 2)]
-                       + [(i, i - 2) for i in range(3, tiles, 2)])
+    gfeat, gframe, near, far = feature_part(half.reshape(1), kgs, gf, wbwd, taps)
+    hopped = lax.ppermute(far, TILE, [(i, i - 2) for i in range(2, tiles, 2)]
+                          + [(i, i + 2) for i in range(1, tiles - 2, 2)])
+    rims = lax.ppermute(jnp.stack([near, hopped]), TILE, [(i, i ^ 1) for i in range(tiles)])
+    near, far = rims[0], rims[1]
     terms = lax.all_to_all(fan(terms, line, F32), LINE, 0, 0)
     total = lax.all_to_all(fan(terms, plane, GATHER_TYPE), PLANE, 0, 0)
     from_up = jnp.where(half == 0, far, near).astype(F32)

time: 103 us -> 103 us (level)
  waiting for transfers between devices: 31.3 us -> 27.4 us
  local copies, waits for them, and re-layouts: 2.66 us -> 5.06 us
  starting transfers between devices: 51.9 us -> 53.3 us
    ppermute x2, waiting for transfers between devices: 0.01 us -> 7.64 us  [the longest x1 3.94 us: step(): lax.ppermute(jnp.stack([near, hopped]), TILE, [(i, i ^ 1) for i in range(...]
    all_to_all x1, waiting for transfers between devices: 5.58 us -> 0.01 us  [step(): terms = lax.all_to_all(parts, PLANE, 0, 0)]
    all_to_all x1, waiting for transfers between devices: 12 us -> 8.03 us  [step(): terms = lax.all_to_all(fan(terms, line, F32), LINE, 0, 0)]
    all_to_all x1, starting transfers between devices: 6.33 us -> 9.98 us  [step(): total = lax.all_to_all(fan(terms, plane, GATHER_TYPE), PLANE, 0, 0)]
    ppermute x2, starting transfers between devices: 9.33 us -> 5.85 us  [the longest x1 4.55 us: step(): lax.ppermute(jnp.stack([near, hopped]), TILE, [(i, i ^ 1) for i in range(...]
    unnamed x8, local copies, waits for them, and re-layouts: 1.14 us -> 3.54 us
    all_to_all x1, starting transfers between devices: 8.62 us -> 11 us  [step(): terms = lax.all_to_all(parts, PLANE, 0, 0)]
    ppermute x1, waiting for transfers between devices: 6.65 us -> 4.79 us  [step(): halo_dn = lax.ppermute(first, TILE, up)]
  transfers between devices with their start and end apart: 7 -> 7, of which waited for: 4 -> 5; matrix products, arithmetic and copies ran while one was open for 3% -> 3% of each run, Pallas kernels for 5% -> 5%
where the time goes in v2:
time: 103 us
  starting transfers between devices  53.3 us (52%)
  waiting for transfers between devices  27.4 us (27%)
  Pallas kernels  15.3 us (15%)
  local copies, waits for them, and re-layouts  5.06 us (5%)
    ppermute x1, starting transfers between devices, step(): halo_up = lax.ppermute(last, TILE, down)  16.3 us
    pallas_call x5, Pallas kernels, vmem_call(): pl.pallas_call(kernel, out_shape=[jax.ShapeDtypeStruct(*o) for o in outs]...  12.9 us
    all_to_all x1, starting transfers between devices, step(): terms = lax.all_to_all(parts, PLANE, 0, 0)  11 us
    all_to_all x1, starting transfers between devices, step(): total = lax.all_to_all(fan(terms, plane, GATHER_TYPE), PLANE, 0, 0)  9.98 us
    all_to_all x1, starting transfers between devices, step(): terms = lax.all_to_all(fan(terms, line, F32), LINE, 0, 0)  8.92 us
    all_to_all x1, waiting for transfers between devices, step(): terms = lax.all_to_all(fan(terms, line, F32), LINE, 0, 0)  8.03 us
    all_to_all x1, waiting for transfers between devices, step(): total = lax.all_to_all(fan(terms, plane, GATHER_TYPE), PLANE, 0, 0)  6.97 us
    ppermute x1, waiting for transfers between devices, step(): halo_dn = lax.ppermute(first, TILE, up)  4.79 us
  transfers between devices with their start and end apart: 7, of which 5 were waited for; matrix products, arithmetic and copies ran while one was open for 3% of the time, Pallas kernels for 5%

profile of v2, /device:TPU:1, one launch (start us, length us, event | category | flops | bytes accessed | tf_op | source)
XLA Modules:
  0.0 102.8 jit_solution(3957043614403464645)
XLA Ops:
  0.6 1.7 %shard_map.67 = (bf16[142,128]{1,0:T(8,128)(2,1)}, bf16[142,128]{1,0:T(8,128)(2,1)}) custom-call(bf16[64,16,128]{2,1,0:T(8,128)(2,1)} %bitcast.25, bf16[2,3,16,128]{3,2,1,0:T(8,128)(2,1)} %bitcast.31), custom_call_target="tpu_custom_call" | custom-call | tf_op jit(solution)/shard_map/pallas_call | solution.py:303
  2.3 16.3 %collective-permute-start = (bf16[142,128]{1,0:T(8,128)(2,1)}, bf16[142,128]{1,0:T(8,128)(2,1)S(1)}, u32[]{:S(2)}, u32[]{:S(2)}) collective-permute-start(bf16[142,128]{1,0:T(8,128)(2,1)} %get-tuple-element.17), channel_id=1, source_target_pairs={{0,1},{1,2},{2,3},{3,4},{4,5},{5,6},{6,7},{8,9},{9,10},{10,11},{11... | collective-permute-start | bytes 109064 | tf_op jit(solution)/shard_map/ppermute | solution.py:347
  18.6 1.3 %collective-permute-start.1 = (bf16[142,128]{1,0:T(8,128)(2,1)}, bf16[142,128]{1,0:T(8,128)(2,1)S(1)}, u32[]{:S(2)}, u32[]{:S(2)}) collective-permute-start(bf16[142,128]{1,0:T(8,128)(2,1)} %get-tuple-element.18), channel_id=1, source_target_pairs={{1,0},{2,1},{3,2},{4,3},{5,4},{6,5},{7,6},{9,8},{10,9},{11,10},{12... | collective-permute-start | bytes 109064 | tf_op jit(solution)/shard_map/ppermute | solution.py:348
  19.9 1.0 reshape.44
  20.9 0.0 copy-start
  20.9 0.9 copy-done
  21.8 0.0 copy-start.1
  21.8 0.7 copy-done.1
  22.6 0.7 copy-done.2
  23.3 4.1 %shard_map.68 = (bf16[16,192,128]{2,1,0:T(8,128)(2,1)S(1)}, bf16[14,2,128,256]{3,2,1,0:T(8,128)(2,1)S(1)}, bf16[14,2,192,128]{3,2,1,0:T(8,128)(2,1)S(1)}, f32[6,48,128]{2,1,0:T(8,128)S(1)}, f32[6,48,128]{2,1,0:T(8,128)S(1)}) custom-call(bf16[64,16,128]{2,1,0:T(8,128)(2,1)S(1)} %bitcast.26, bf16[2,3,16,128]{3,2,1,0:T(8,128)(2,1)S(1)} %bitcast.32, ...), custom_call_target="tpu_custom_call" | custom-call | tf_op jit(solution)/shard_map/pallas_call | solution.py:250
  27.4 0.0 collective-permute-done.halo_up
  27.4 4.8 %collective-permute-done.1.halo_dn = bf16[142,128]{1,0:T(8,128)(2,1)S(1)} collective-permute-done((bf16[142,128]{1,0:T(8,128)(2,1)}, bf16[142,128]{1,0:T(8,128)(2,1)S(1)}, u32[]{:S(2)}, u32[]{:S(2)}) %collective-permute-start.1) | collective-permute-done | bytes 36384 | tf_op jit(solution)/shard_map/ppermute | solution.py:348
  32.2 6.7 %shard_map.69 = (f32[32,16,128]{2,1,0:T(8,128)}, bf16[16,128,128]{2,1,0:T(8,128)(2,1)S(1)}, f32[6,48,128]{2,1,0:T(8,128)S(1)}) custom-call(bf16[142,128]{1,0:T(8,128)(2,1)S(1)} %collective-permute-done.halo_up, bf16[142,128]{1,0:T(8,128)(2,1)S(1)} %collective-permute-done.1.halo_dn, f32[3,16,128]{2,1,0:T(8,128)S(1)} %bitcast.30, ...), custom_call_target="tpu_custom_call" | custom-call | tf_op jit(solution)/shard_map/pallas_call | solution.py:250
  38.9 11.0 %all-to-all-start = ((f32[32,16,128]{2,1,0:T(8,128)}), f32[32,16,128]{2,1,0:T(8,128)S(1)}, u32[]{:S(2)}, u32[]{:S(2)}) async-start(f32[32,16,128]{2,1,0:T(8,128)} %get-tuple-element.24), calls=%async_computation | async-start | bytes 524288 | tf_op jit(solution)/shard_map/all_to_all | solution.py:353
  49.9 0.2 reshape_reshape.3
  50.1 0.3 copy.8
  50.4 0.7 shard_map.73
  51.2 1.3 %collective-permute-start.2 = (bf16[142,128]{1,0:T(8,128)(2,1)S(1)}, bf16[142,128]{1,0:T(8,128)(2,1)S(1)}, u32[]{:S(2)}, u32[]{:S(2)}) collective-permute-start(bf16[142,128]{1,0:T(8,128)(2,1)S(1)} %get-tuple-element.29), channel_id=1, source_target_pairs={{2,0},{4,2},{6,4},{1,3},{3,5},{5,7},{10,8},{12,10},{14,12},{9,11},... | collective-permute-start | bytes 109064 | tf_op jit(solution)/shard_map/ppermute | solution.py:356
  52.5 3.7 %collective-permute-done.2 = bf16[142,128]{1,0:T(8,128)(2,1)S(1)} collective-permute-done((bf16[142,128]{1,0:T(8,128)(2,1)S(1)}, bf16[142,128]{1,0:T(8,128)(2,1)S(1)}, u32[]{:S(2)}, u32[]{:S(2)}) %collective-permute-start.2) | collective-permute-done | bytes 36384 | tf_op jit(solution)/shard_map/ppermute | solution.py:356
  56.2 4.6 %collective-permute-start.3 = (bf16[2,142,128]{2,1,0:T(8,128)(2,1)S(1)}, bf16[2,142,128]{2,1,0:T(8,128)(2,1)S(1)}, u32[]{:S(2)}, u32[]{:S(2)}) collective-permute-start(bf16[2,142,128]{2,1,0:T(8,128)(2,1)S(1)} %pad_maximum_fusion), channel_id=1, source_target_pairs={{0,1},{1,0},{2,3},{3,2},{4,5},{5,4},{6,7},{7,6},{8,9},{9,8},{10,11... | collective-permute-start | bytes 218120 | tf_op jit(solution)/shard_map/ppermute | solution.py:358
  60.8 0.0 all-to-all-done.parts_ref
  60.8 0.7 shard_map.70
  61.5 8.9 %all-to-all-start.1 = ((f32[16,16,128]{2,1,0:T(8,128)}), f32[16,16,128]{2,1,0:T(8,128)S(1)}, u32[]{:S(2)}, u32[]{:S(2)}) async-start(f32[16,16,128]{2,1,0:T(8,128)} %shard_map.70), calls=%async_computation.1 | async-start | bytes 262144 | tf_op jit(solution)/shard_map/all_to_all | solution.py:360
  70.4 3.9 %collective-permute-done.3 = bf16[2,142,128]{2,1,0:T(8,128)(2,1)S(1)} collective-permute-done((bf16[2,142,128]{2,1,0:T(8,128)(2,1)S(1)}, bf16[2,142,128]{2,1,0:T(8,128)(2,1)S(1)}, u32[]{:S(2)}, u32[]{:S(2)}) %collective-permute-start.3) | collective-permute-done | bytes 72736 | tf_op jit(solution)/shard_map/ppermute | solution.py:358
  74.4 0.2 fusion.1
  74.6 1.1 %copy.10 = f32[1,64,16,128]{3,2,1,0:T(8,128)} copy(f32[1,64,16,128]{3,1,2,0:T(8,128)S(1)} %fusion.1) | data formatting | bytes 1048576
  75.7 8.0 %all-to-all-done.1.parts_ref = f32[16,16,128]{2,1,0:T(8,128)S(1)} async-done(((f32[16,16,128]{2,1,0:T(8,128)}), f32[16,16,128]{2,1,0:T(8,128)S(1)}, u32[]{:S(2)}, u32[]{:S(2)}) %all-to-all-start.1) | async-done | bytes 131104 | tf_op jit(solution)/shard_map/all_to_all | solution.py:360
  83.7 0.7 shard_map.71
  84.4 10.0 %all-to-all-start.2 = ((bf16[32,16,128]{2,1,0:T(8,128)(2,1)}), bf16[32,16,128]{2,1,0:T(8,128)(2,1)S(1)}, u32[]{:S(2)}, u32[]{:S(2)}) async-start(bf16[32,16,128]{2,1,0:T(8,128)(2,1)} %shard_map.71), calls=%async_computation.2 | async-start | bytes 262144 | tf_op jit(solution)/shard_map/all_to_all | solution.py:361
  94.4 0.6 pad_add_fusion
  95.0 7.0 %all-to-all-done.2.parts = bf16[32,16,128]{2,1,0:T(8,128)(2,1)S(1)} async-done(((bf16[32,16,128]{2,1,0:T(8,128)(2,1)}), bf16[32,16,128]{2,1,0:T(8,128)(2,1)S(1)}, u32[]{:S(2)}, u32[]{:S(2)}) %all-to-all-start.2) | async-done | bytes 131104 | tf_op jit(solution)/shard_map/all_to_all | solution.py:361
  102.0 0.8 shard_map.72
  (11 shorter events, 0.1 us)
Async XLA Ops:
  2.3 25.1 %collective-permute-start = (bf16[142,128]{1,0:T(8,128)(2,1)}, bf16[142,128]{1,0:T(8,128)(2,1)S(1)}, u32[]{:S(2)}, u32[]{:S(2)}) collective-permute-start(bf16[142,128]{1,0:T(8,128)(2,1)} %get-tuple-element.17), channel_id=1, source_target_pairs={{0,1},{1,2},{2,3},{3,4},{4,5},{5,6},{6,7},{8,9},{9,10},{10,11},{11... | collective-permute-start | bytes 109064 | tf_op jit(solution)/shard_map/ppermute | solution.py:347
  18.6 13.6 %collective-permute-start.1 = (bf16[142,128]{1,0:T(8,128)(2,1)}, bf16[142,128]{1,0:T(8,128)(2,1)S(1)}, u32[]{:S(2)}, u32[]{:S(2)}) collective-permute-start(bf16[142,128]{1,0:T(8,128)(2,1)} %get-tuple-element.18), channel_id=1, source_target_pairs={{1,0},{2,1},{3,2},{4,3},{5,4},{6,5},{7,6},{9,8},{10,9},{11,10},{12... | collective-permute-start | bytes 109064 | tf_op jit(solution)/shard_map/ppermute | solution.py:348
  20.9 1.0 copy-start
  21.8 0.7 copy-start.1
  22.6 0.7 copy-start.2
  38.9 21.9 %all-to-all-start = ((f32[32,16,128]{2,1,0:T(8,128)}), f32[32,16,128]{2,1,0:T(8,128)S(1)}, u32[]{:S(2)}, u32[]{:S(2)}) async-start(f32[32,16,128]{2,1,0:T(8,128)} %get-tuple-element.24), calls=%async_computation | async-start | bytes 524288 | tf_op jit(solution)/shard_map/all_to_all | solution.py:353
  51.2 5.0 %collective-permute-start.2 = (bf16[142,128]{1,0:T(8,128)(2,1)S(1)}, bf16[142,128]{1,0:T(8,128)(2,1)S(1)}, u32[]{:S(2)}, u32[]{:S(2)}) collective-permute-start(bf16[142,128]{1,0:T(8,128)(2,1)S(1)} %get-tuple-element.29), channel_id=1, source_target_pairs={{2,0},{4,2},{6,4},{1,3},{3,5},{5,7},{10,8},{12,10},{14,12},{9,11},... | collective-permute-start | bytes 109064 | tf_op jit(solution)/shard_map/ppermute | solution.py:356
  56.2 18.1 %collective-permute-start.3 = (bf16[2,142,128]{2,1,0:T(8,128)(2,1)S(1)}, bf16[2,142,128]{2,1,0:T(8,128)(2,1)S(1)}, u32[]{:S(2)}, u32[]{:S(2)}) collective-permute-start(bf16[2,142,128]{2,1,0:T(8,128)(2,1)S(1)} %pad_maximum_fusion), channel_id=1, source_target_pairs={{0,1},{1,0},{2,3},{3,2},{4,5},{5,4},{6,7},{7,6},{8,9},{9,8},{10,11... | collective-permute-start | bytes 218120 | tf_op jit(solution)/shard_map/ppermute | solution.py:358
  61.5 22.3 %all-to-all-start.1 = ((f32[16,16,128]{2,1,0:T(8,128)}), f32[16,16,128]{2,1,0:T(8,128)S(1)}, u32[]{:S(2)}, u32[]{:S(2)}) async-start(f32[16,16,128]{2,1,0:T(8,128)} %shard_map.70), calls=%async_computation.1 | async-start | bytes 262144 | tf_op jit(solution)/shard_map/all_to_all | solution.py:360
  84.4 17.6 %all-to-all-start.2 = ((bf16[32,16,128]{2,1,0:T(8,128)(2,1)}), bf16[32,16,128]{2,1,0:T(8,128)(2,1)S(1)}, u32[]{:S(2)}, u32[]{:S(2)}) async-start(bf16[32,16,128]{2,1,0:T(8,128)(2,1)} %shard_map.71), calls=%async_computation.2 | async-start | bytes 262144 | tf_op jit(solution)/shard_map/all_to_all | solution.py:361

commit v3 on v1

--- a/solution.py
+++ b/solution.py
@@ -219,10 +219,11 @@
     out[:, 128 * full:] = jnp.concatenate([tail[:, :64], tail[:, 64:]], 0)
 
 
-def halo_kernel(taps, feat_hbm, frames_hbm, first, last, feat, frames, fs, sems):
+def halo_kernel(taps, feat_hbm, frames_hbm, cot_hbm, first, last, feat, frames, cot, fs, sems):
     rim = (taps - 1) // 2
     copies = [pltpu.make_async_copy(feat_hbm, feat, sems.at[0]),
-              pltpu.make_async_copy(frames_hbm, frames, sems.at[1])]
+              pltpu.make_async_copy(frames_hbm, frames, sems.at[1]),
+              pltpu.make_async_copy(cot_hbm, cot, sems.at[2])]
     for copy in copies:
         copy.start()
     for copy in copies:
@@ -236,6 +237,23 @@
         at = channels + n * rim
         first[at:at + rim] = frame[:rim].astype(BF16)
         last[at:at + rim] = frame[rows - rim:].astype(BF16)
+
+
+def finish_kernel(taps, half, gfeat, gframe, near, far, out_feat, out_frame, rims):
+    rim = (taps - 1) // 2
+    channels = near.shape[0] - 6 * rim
+    rows = gframe.shape[1]
+    rims[0] = near[...].astype(F32)
+    rims[1] = far[...].astype(F32)
+    up, dn = 1 - half[0], half[0]
+    out_feat[...] = gfeat[...]
+    out_feat[pl.ds(0, channels, stride=rows), :] += rims[up, :channels]
+    out_feat[pl.ds(rows - 1, channels, stride=rows), :] += rims[dn, :channels]
+    out_frame[...] = gframe[...]
+    for n in range(6):
+        at = channels + n * rim
+        out_frame[n, :rim] += rims[up, at:at + rim]
+        out_frame[n, rows - rim:] += rims[dn, at:at + rim]
 
 
 def order(hw, taps):
@@ -292,18 +310,32 @@
     )(half, kgs, gf, wbwd)
 
 
-def halo_rows(feat, frames, taps):
+def halo_rows(feat, frames, cot, taps):
     channels, rows, width = feat.shape
-    shape = ((channels + 3 * (taps - 1), width), BF16)
+    shape = (channels + 3 * (taps - 1), width)
     hbm, vm = pl.BlockSpec(memory_space=pltpu.HBM), pl.BlockSpec(memory_space=pltpu.VMEM)
+    held = [pltpu.with_memory_space_constraint(v, pltpu.HBM) for v in (feat, frames, cot)]
     return pl.pallas_call(
         functools.partial(halo_kernel, taps),
-        out_shape=[jax.ShapeDtypeStruct(*shape)] * 2,
-        in_specs=[hbm, hbm],
-        out_specs=[vm, vm],
-        scratch_shapes=[pltpu.VMEM(feat.shape, BF16), pltpu.VMEM(frames.shape, BF16),
-                        pltpu.VMEM((channels * rows, width), F32), pltpu.SemaphoreType.DMA((2,))],
-    )(feat, frames)
+        out_shape=[jax.ShapeDtypeStruct(shape, BF16)] * 2
+        + [jax.ShapeDtypeStruct(v.shape, v.dtype) for v in (feat, frames, cot)],
+        in_specs=[hbm] * 3,
+        out_specs=[vm] * 5,
+        scratch_shapes=[pltpu.VMEM((channels * rows, width), F32), pltpu.SemaphoreType.DMA((3,))],
+        compiler_params=pltpu.CompilerParams(vmem_limit_bytes=VMEM_GRANT),
+    )(*held)
+
+
+def finish(half, gfeat, gframe, near, far, taps):
+    vm = pl.BlockSpec(memory_space=pltpu.VMEM)
+    return pl.pallas_call(
+        functools.partial(finish_kernel, taps),
+        out_shape=[jax.ShapeDtypeStruct(v.shape, F32) for v in (gfeat, gframe)],
+        in_specs=[pl.BlockSpec(memory_space=pltpu.SMEM)] + [vm] * 4,
+        out_specs=[vm] * 2,
+        scratch_shapes=[pltpu.VMEM((2,) + near.shape, F32)],
+        compiler_params=pltpu.CompilerParams(vmem_limit_bytes=VMEM_GRANT),
+    )(half, gfeat, gframe, near, far)
 
 
 def both_weights(hw, taps, channels):
@@ -332,14 +364,13 @@
 
 def step(frames, features, cotangent, head_weight):
     taps = head_weight.shape[0] // 4
-    rim = (taps - 1) // 2
     feat, frame, cot = features[0], frames[0], cotangent[0]
     channels, rows, width = feat.shape
     tiles, plane, line = lax.axis_size(TILE), lax.axis_size(PLANE), lax.axis_size(LINE)
     down = [(i, i + 1) for i in range(tiles - 1)]
     up = [(i + 1, i) for i in range(tiles - 1)]
 
-    first, last = halo_rows(feat, frame, taps)
+    first, last, feat, frame, cot = halo_rows(feat, frame, cot, taps)
     halo_up = lax.ppermute(last, TILE, down)
     halo_dn = lax.ppermute(first, TILE, up)
     wfwd, wbwd = both_weights(head_weight, taps, channels)
@@ -355,18 +386,11 @@
                        + [(i, i - 2) for i in range(3, tiles, 2)])
     terms = lax.all_to_all(fan(terms, line, F32), LINE, 0, 0)
     total = lax.all_to_all(fan(terms, plane, GATHER_TYPE), PLANE, 0, 0)
-    from_up = jnp.where(half == 0, far, near).astype(F32)
-    from_dn = jnp.where(half == 0, near, far).astype(F32)
     pixels = plane * line * rows * width
     grad_weight = unpack(total, taps, 9 * channels, pixels ** -0.5)
-
-    gfeat = gfeat.reshape(channels, rows, width)
-    gfeat = (gfeat + jnp.pad(from_up[:channels, None], ((0, 0), (0, rows - 1), (0, 0)))
-             + jnp.pad(from_dn[:channels, None], ((0, 0), (rows - 1, 0), (0, 0))))
-    gframe = (gframe
-              + jnp.pad(from_up[channels:].reshape(6, rim, width), ((0, 0), (0, rows - rim), (0, 0)))
-              + jnp.pad(from_dn[channels:].reshape(6, rim, width), ((0, 0), (rows - rim, 0), (0, 0))))
-    return grad_weight, gfeat[None], gframe.reshape(1, 2, 3, rows, width)
+    gfeat, gframe = finish(half.reshape(1), gfeat, gframe, near, far, taps)
+    return (grad_weight, gfeat.reshape(1, channels, rows, width),
+            gframe.reshape(1, 2, 3, rows, width))
 
 
 def solution(mesh):

time: 103 us -> 91.9 us (0.89)
  waiting for transfers between devices: 31.3 us -> 10.5 us
  blocking collectives: 0 us -> 19.7 us
  starting transfers between devices: 51.9 us -> 44.2 us
  local copies, waits for them, and re-layouts: 2.66 us -> 1.52 us
    all_to_all x0 -> x1, blocking collectives: none -> 19.7 us  [step(): terms = lax.all_to_all(parts, PLANE, 0, 0)]
    all_to_all x1, waiting for transfers between devices: 12 us -> 0.01 us  [step(): terms = lax.all_to_all(fan(terms, line, F32), LINE, 0, 0)]
    all_to_all x1 -> x0, starting transfers between devices: 8.62 us -> none  [step(): terms = lax.all_to_all(parts, PLANE, 0, 0)]
    all_to_all x1, starting transfers between devices: 10.1 us -> 3.51 us  [step(): terms = lax.all_to_all(fan(terms, line, F32), LINE, 0, 0)]
    ppermute x1, starting transfers between devices: 6.07 us -> 11.9 us  [step(): rims = lax.ppermute(rims, TILE, [(i, i ^ 1) for i in range(tiles)])]
    all_to_all x1 -> x0, waiting for transfers between devices: 5.58 us -> none  [step(): terms = lax.all_to_all(parts, PLANE, 0, 0)]
    all_to_all x1, waiting for transfers between devices: 7.06 us -> 2.47 us  [step(): total = lax.all_to_all(fan(terms, plane, GATHER_TYPE), PLANE, 0, 0)]
    all_to_all x1, starting transfers between devices: 6.33 us -> 7.96 us  [step(): total = lax.all_to_all(fan(terms, plane, GATHER_TYPE), PLANE, 0, 0)]
  transfers between devices with their start and end apart: 7 -> 6, of which waited for: 4 -> 3; matrix products, arithmetic and copies ran while one was open for 3% -> 2% of each run, Pallas kernels for 5% -> 7%
where the time goes in v3:
time: 91.9 us; the launch traced here: 91.5 us
  starting transfers between devices  44.2 us (48%)
  blocking collectives  19.7 us (21%)
  Pallas kernels  14.9 us (16%)
  waiting for transfers between devices  10.5 us (11%)
  local copies, waits for them, and re-layouts  1.52 us (2%)
    all_to_all x1, blocking collectives, step(): terms = lax.all_to_all(parts, PLANE, 0, 0)  19.7 us
    ppermute x1, starting transfers between devices, step(): halo_up = lax.ppermute(last, TILE, down)  16.3 us
    pallas_call x5, Pallas kernels, vmem_call(): pl.pallas_call(kernel, out_shape=[jax.ShapeDtypeStruct(*o) for o in outs]...  12.2 us
    ppermute x1, starting transfers between devices, step(): rims = lax.ppermute(rims, TILE, [(i, i ^ 1) for i in range(tiles)])  11.9 us
    all_to_all x1, starting transfers between devices, step(): total = lax.all_to_all(fan(terms, plane, GATHER_TYPE), PLANE, 0, 0)  7.96 us
    ppermute x1, waiting for transfers between devices, step(): halo_dn = lax.ppermute(first, TILE, up)  7.01 us
    all_to_all x1, starting transfers between devices, step(): terms = lax.all_to_all(fan(terms, line, F32), LINE, 0, 0)  3.51 us
    ppermute x1, starting transfers between devices, step(): lax.ppermute(rims[1], TILE, [(i, i + 2) for i in range(0, tiles - 2, 2)]...  3.26 us
  transfers between devices with their start and end apart: 6, of which 3 were waited for; matrix products, arithmetic and copies ran while one was open for 2% of the time, Pallas kernels for 7%

profile of v3, /device:TPU:1, one launch (start us, length us, event | category | flops | bytes accessed | tf_op | source)
XLA Modules:
  0.0 91.5 jit_solution(17176716068788531496)
XLA Ops:
  0.6 1.1 %shard_map.67 = (bf16[142,128]{1,0:T(8,128)(2,1)S(1)}, bf16[142,128]{1,0:T(8,128)(2,1)S(1)}, bf16[64,16,128]{2,1,0:T(8,128)(2,1)S(1)}, bf16[2,3,16,128]{3,2,1,0:T(8,128)(2,1)S(1)}, f32[3,16,128]{2,1,0:T(8,128)S(1)}) custom-call(bf16[64,16,128]{2,1,0:T(8,128)(2,1)} %bitcast.24, bf16[2,3,16,128]{3,2,1,0:T(8,128)(2,1)} %bitcast.25, f32[3,16,128]{2,1,0:T(8,128)} %bitcast.26), custom_call_target="tpu_custom_call" | custom-call | tf_op jit(solution)/shard_map/pallas_call | solution.py:318
  1.7 16.3 %collective-permute-start = (bf16[142,128]{1,0:T(8,128)(2,1)S(1)}, bf16[142,128]{1,0:T(8,128)(2,1)S(1)}, u32[]{:S(2)}, u32[]{:S(2)}) collective-permute-start(bf16[142,128]{1,0:T(8,128)(2,1)S(1)} %get-tuple-element.21), channel_id=1, source_target_pairs={{0,1},{1,2},{2,3},{3,4},{4,5},{5,6},{6,7},{8,9},{9,10},{10,11},{11... | collective-permute-start | bytes 109064 | tf_op jit(solution)/shard_map/ppermute | solution.py:374
  18.0 1.3 %collective-permute-start.1 = (bf16[142,128]{1,0:T(8,128)(2,1)S(1)}, bf16[142,128]{1,0:T(8,128)(2,1)S(1)}, u32[]{:S(2)}, u32[]{:S(2)}) collective-permute-start(bf16[142,128]{1,0:T(8,128)(2,1)S(1)} %get-tuple-element.22), channel_id=1, source_target_pairs={{1,0},{2,1},{3,2},{4,3},{5,4},{6,5},{7,6},{9,8},{10,9},{11,10},{12... | collective-permute-start | bytes 109064 | tf_op jit(solution)/shard_map/ppermute | solution.py:375
  19.3 1.0 %reshape.25 = bf16[2,2,27,576]{3,2,1,0:T(8,128)(2,1)S(1)} reshape(bf16[108,576]{1,0:T(8,128)(2,1)} %param.7) | data formatting | bytes 248832 | tf_op jit(solution)/shard_map/reshape | solution.py:260
  20.3 4.1 %shard_map.68 = (bf16[16,192,128]{2,1,0:T(8,128)(2,1)S(1)}, bf16[14,2,128,256]{3,2,1,0:T(8,128)(2,1)S(1)}, bf16[14,2,192,128]{3,2,1,0:T(8,128)(2,1)S(1)}, f32[6,48,128]{2,1,0:T(8,128)S(1)}, f32[6,48,128]{2,1,0:T(8,128)S(1)}) custom-call(bf16[64,16,128]{2,1,0:T(8,128)(2,1)S(1)} %get-tuple-element.24.feat, ...), custom_call_target="tpu_custom_call" | custom-call | tf_op jit(solution)/shard_map/pallas_call | solution.py:266
  24.4 0.0 collective-permute-done.halo_up
  24.4 7.0 %collective-permute-done.1.halo_dn = bf16[142,128]{1,0:T(8,128)(2,1)S(1)} collective-permute-done((bf16[142,128]{1,0:T(8,128)(2,1)S(1)}, bf16[142,128]{1,0:T(8,128)(2,1)S(1)}, u32[]{:S(2)}, u32[]{:S(2)}) %collective-permute-start.1) | collective-permute-done | bytes 36384 | tf_op jit(solution)/shard_map/ppermute | solution.py:375
  31.4 6.0 %shard_map.69 = (f32[32,16,128]{2,1,0:T(8,128)S(1)}, bf16[16,128,128]{2,1,0:T(8,128)(2,1)S(1)}, f32[6,48,128]{2,1,0:T(8,128)S(1)}) custom-call(bf16[142,128]{1,0:T(8,128)(2,1)S(1)} %collective-permute-done.halo_up, bf16[142,128]{1,0:T(8,128)(2,1)S(1)} %collective-permute-done.1.halo_dn, f32[3,16,128]{2,1,0:T(8,128)S(1)} %get-tuple-element.23.cot, ...), custom_call_target="tpu_custom_call" | custom-call | tf_op jit(solution)/shard_map/pallas_call | solution.py:266
  37.3 19.7 %all_to_all.15.parts_ref = f32[32,16,128]{2,1,0:T(8,128)S(1)} all-to-all(f32[32,16,128]{2,1,0:T(8,128)S(1)} %get-tuple-element.31), channel_id=1, replica_groups=mesh['zl'=8,'y'=4,'core'=2,'x'=4,'zh'=2] {'y','core','x'}, dimensions={0} | all-to-all | bytes 524288 | tf_op jit(solution)/shard_map/all_to_all | solution.py:380
  57.0 0.7 shard_map.70
  57.7 3.5 %all-to-all-start.1 = ((f32[16,16,128]{2,1,0:T(8,128)}), f32[16,16,128]{2,1,0:T(8,128)S(1)}, u32[]{:S(2)}, u32[]{:S(2)}) async-start(f32[16,16,128]{2,1,0:T(8,128)} %shard_map.70), calls=%async_computation.1 | async-start | bytes 262144 | tf_op jit(solution)/shard_map/all_to_all | solution.py:387
  61.2 0.2 reshape_reshape.3
  61.5 0.3 copy.7
  61.8 0.7 shard_map.73
  62.5 11.9 %collective-permute-start.2 = (bf16[2,142,128]{2,1,0:T(8,128)(2,1)S(1)}, bf16[2,142,128]{2,1,0:T(8,128)(2,1)S(1)}, u32[]{:S(2)}, u32[]{:S(2)}) collective-permute-start(bf16[2,142,128]{2,1,0:T(8,128)(2,1)S(1)} %get-tuple-element.36), channel_id=1, source_target_pairs={{0,1},{1,0},{2,3},{3,2},{4,5},{5,4},{6,7},{7,6},{8,9},{9,8},{10,11... | collective-permute-start | bytes 218120 | tf_op jit(solution)/shard_map/ppermute | solution.py:383
  74.4 0.0 all-to-all-done.1.parts_ref
  74.4 0.7 shard_map.71
  75.1 8.0 %all-to-all-start.2 = ((bf16[32,16,128]{2,1,0:T(8,128)(2,1)}), bf16[32,16,128]{2,1,0:T(8,128)(2,1)S(1)}, u32[]{:S(2)}, u32[]{:S(2)}) async-start(bf16[32,16,128]{2,1,0:T(8,128)(2,1)} %shard_map.71), calls=%async_computation.2 | async-start | bytes 262144 | tf_op jit(solution)/shard_map/all_to_all | solution.py:388
  83.1 0.0 collective-permute-done.2
  83.1 3.3 %collective-permute-start.3 = (bf16[142,128]{1,0:T(8,128)(2,1)S(1)}, bf16[142,128]{1,0:T(8,128)(2,1)S(1)}, u32[]{:S(2)}, u32[]{:S(2)}) collective-permute-start(bf16[142,128]{1,0:T(8,128)(2,1)S(1)} %get-tuple-element.39), channel_id=1, source_target_pairs={{0,2},{2,4},{4,6},{3,1},{5,3},{7,5},{8,10},{10,12},{12,14},{11,9},... | collective-permute-start | bytes 109064 | tf_op jit(solution)/shard_map/ppermute | solution.py:385
  86.4 1.0 %collective-permute-done.3.far = bf16[142,128]{1,0:T(8,128)(2,1)S(1)} collective-permute-done((bf16[142,128]{1,0:T(8,128)(2,1)S(1)}, bf16[142,128]{1,0:T(8,128)(2,1)S(1)}, u32[]{:S(2)}, u32[]{:S(2)}) %collective-permute-start.3) | collective-permute-done | bytes 36384 | tf_op jit(solution)/shard_map/ppermute | solution.py:385
  87.4 0.9 shard_map.74
  88.3 2.5 %all-to-all-done.2.parts = bf16[32,16,128]{2,1,0:T(8,128)(2,1)S(1)} async-done(((bf16[32,16,128]{2,1,0:T(8,128)(2,1)}), bf16[32,16,128]{2,1,0:T(8,128)(2,1)S(1)}, u32[]{:S(2)}, u32[]{:S(2)}) %all-to-all-start.2) | async-done | bytes 131104 | tf_op jit(solution)/shard_map/all_to_all | solution.py:388
  90.8 0.8 shard_map.72
  (4 shorter events, 0.1 us)
Async XLA Ops:
  1.7 22.7 %collective-permute-start = (bf16[142,128]{1,0:T(8,128)(2,1)S(1)}, bf16[142,128]{1,0:T(8,128)(2,1)S(1)}, u32[]{:S(2)}, u32[]{:S(2)}) collective-permute-start(bf16[142,128]{1,0:T(8,128)(2,1)S(1)} %get-tuple-element.21), channel_id=1, source_target_pairs={{0,1},{1,2},{2,3},{3,4},{4,5},{5,6},{6,7},{8,9},{9,10},{10,11},{11... | collective-permute-start | bytes 109064 | tf_op jit(solution)/shard_map/ppermute | solution.py:374
  18.0 13.4 %collective-permute-start.1 = (bf16[142,128]{1,0:T(8,128)(2,1)S(1)}, bf16[142,128]{1,0:T(8,128)(2,1)S(1)}, u32[]{:S(2)}, u32[]{:S(2)}) collective-permute-start(bf16[142,128]{1,0:T(8,128)(2,1)S(1)} %get-tuple-element.22), channel_id=1, source_target_pairs={{1,0},{2,1},{3,2},{4,3},{5,4},{6,5},{7,6},{9,8},{10,9},{11,10},{12... | collective-permute-start | bytes 109064 | tf_op jit(solution)/shard_map/ppermute | solution.py:375
  57.7 16.7 %all-to-all-start.1 = ((f32[16,16,128]{2,1,0:T(8,128)}), f32[16,16,128]{2,1,0:T(8,128)S(1)}, u32[]{:S(2)}, u32[]{:S(2)}) async-start(f32[16,16,128]{2,1,0:T(8,128)} %shard_map.70), calls=%async_computation.1 | async-start | bytes 262144 | tf_op jit(solution)/shard_map/all_to_all | solution.py:387
  62.5 20.5 %collective-permute-start.2 = (bf16[2,142,128]{2,1,0:T(8,128)(2,1)S(1)}, bf16[2,142,128]{2,1,0:T(8,128)(2,1)S(1)}, u32[]{:S(2)}, u32[]{:S(2)}) collective-permute-start(bf16[2,142,128]{2,1,0:T(8,128)(2,1)S(1)} %get-tuple-element.36), channel_id=1, source_target_pairs={{0,1},{1,0},{2,3},{3,2},{4,5},{5,4},{6,7},{7,6},{8,9},{9,8},{10,11... | collective-permute-start | bytes 218120 | tf_op jit(solution)/shard_map/ppermute | solution.py:383
  75.1 15.7 %all-to-all-start.2 = ((bf16[32,16,128]{2,1,0:T(8,128)(2,1)}), bf16[32,16,128]{2,1,0:T(8,128)(2,1)S(1)}, u32[]{:S(2)}, u32[]{:S(2)}) async-start(bf16[32,16,128]{2,1,0:T(8,128)(2,1)} %shard_map.71), calls=%async_computation.2 | async-start | bytes 262144 | tf_op jit(solution)/shard_map/all_to_all | solution.py:388
  83.1 4.3 %collective-permute-start.3 = (bf16[142,128]{1,0:T(8,128)(2,1)S(1)}, bf16[142,128]{1,0:T(8,128)(2,1)S(1)}, u32[]{:S(2)}, u32[]{:S(2)}) collective-permute-start(bf16[142,128]{1,0:T(8,128)(2,1)S(1)} %get-tuple-element.39), channel_id=1, source_target_pairs={{0,2},{2,4},{4,6},{3,1},{5,3},{7,5},{8,10},{10,12},{12,14},{11,9},... | collective-permute-start | bytes 109064 | tf_op jit(solution)/shard_map/ppermute | solution.py:385
